TPU v7x, 32 devices: a whole 2x2x4 slice. The times are simulated.
32 devices in a mesh: groups: 2 (over y), gx: 4 (over z), gy: 2 (over core), gz: 2 (over x).
Axes of the slice: x: 2, y: 2, z: 4, core: 2. Of those that a mesh axis runs over, the one named last changes fastest.
Arguments:
- tokens: bfloat16 [6144, 4096], P(('groups', 'gx', 'gz'), 'gy'), parts along dimension 0, may hold values from -6 to 6
- weights: bfloat16 [4096, 14336], P('gy', ('gz', 'gx')), may hold values from -0.09375 to 0.09375
- counts: int32 [8], P(('groups', 'gx')), parts along dimension 0, may hold values from 1 to 6
Outputs:
- projected: bfloat16 [6144, 14336], P(('groups', 'gx', 'gy'), 'gz'), parts along dimension 0
There are 2 independent parts, one for each index of `groups`. A program takes and returns all parts, laid end to end along the dimension named above; an argument that names none is the same for every part. Nothing has to cross between parts.
Inputs may be any that keep to these rules, and one draw needn't show every extreme that they name: counts[s] is the number of whole blocks of 128 rows, at the start of token shard s, that hold valid rows.
All inputs are finite; a program needn't handle non-finite values.
Results may differ from a plain program's by a relative error of at most 0.001.
Values may be sent and summed in bfloat16 or wider, within the bound.
A program may use at most 128 MiB of HBM per device.

v0:
```python
import jax
import jax.numpy as jnp
from jax import lax
from jax.sharding import PartitionSpec as P

BLOCK = 128


def block_product(left_rows, column_piece, valid_count):
    total_rows = left_rows.shape[0]
    row_index = jnp.arange(total_rows, dtype=jnp.int32)
    product = jnp.dot(left_rows, column_piece, preferred_element_type=jnp.float32)
    return jnp.where((row_index < valid_count * BLOCK)[:, None], product, jnp.float32(0.0))


def shards(tokens, weights, counts):
    valid_count = counts[0]
    shard_rows = lax.all_gather(tokens, "gz", axis=0, tiled=True)
    partial_value = block_product(
        shard_rows, lax.all_gather(weights, "gx", axis=1, tiled=True), valid_count
    )
    result = lax.psum_scatter(partial_value, "gy", scatter_dimension=0, tiled=True)
    return result.astype(jnp.bfloat16)


def solution(mesh):
    return jax.shard_map(
        shards,
        mesh=mesh,
        in_specs=(P(("groups", "gx", "gz"), "gy"), P("gy", ("gz", "gx")), P(("groups", "gx"))),
        out_specs=P(("groups", "gx", "gy"), "gz"),
        check_vma=False,
    )
```

profile of v0, /device:TPU:0, one launch (start us, length us, event | category | flops | bytes accessed | tf_op | source)
XLA Modules:
  0.0 622.0 jit_solution(3898355794683110476)
XLA Ops:
  6.5 0.0 all-gather.3.cloned.1.call-start
  6.5 0.7 all-gather.3.cloned.1.call-update
  7.3 0.0 all-gather.5.cloned.1.call-start
  7.3 0.7 all-gather.5.cloned.1.call-update
  8.0 0.0 reduce-scatter.2.cloned.1.call-start
  8.7 47.8 %all-gather.3.cloned.1.call-done = bf16[768,2048]{1,0:T(8,128)(2,1)} async-done(((bf16[384,2048]{1,0:T(8,128)(2,1)}), bf16[768,2048]{1,0:T(8,128)(2,1)}) %all-gather.3.cloned.1.call-update) | async-done | bytes 3145744 | tf_op jit(solution)/shard_map/all_gather | solution.py:18
  56.5 494.7 %all-gather.5.cloned.1.call-done = bf16[2048,7168]{1,0:T(8,128)(2,1)} async-done(((bf16[2048,1792]{1,0:T(8,128)(2,1)}), bf16[2048,7168]{1,0:T(8,128)(2,1)}) %all-gather.5.cloned.1.call-update) | async-done | bytes 29360144 | tf_op jit(solution)/shard_map/all_gather | solution.py:20
  551.2 29.9 %convolution_select_fusion = f32[768,7168]{1,0:T(8,128)} fusion(bf16[768,2048]{1,0:T(8,128)(2,1)} %all-gather.3.cloned.1.call-done, bf16[2048,7168]{1,0:T(8,128)(2,1)} %all-gather.5.cloned.1.call-done, pred[768]{0:T(1024)(128)(4,1)S(1)} %iota_compare_fusion), kind=kOutput, calls=%fused_computation | convolution fusion | flops 22554083328 | bytes 54526720 | tf_op jit(solution)/shard_map/dot_general | solution.py:12
  581.1 0.0 reduce-scatter.2.cloned.1.call-update
  581.2 27.0 %reduce-scatter.2.cloned.1.call-done = f32[384,7168]{1,0:T(8,128)} async-done(((f32[768,7168]{1,0:T(8,128)}), f32[384,7168]{1,0:T(8,128)}) %reduce-scatter.2.cloned.1.call-update) | async-done | bytes 11010064 | tf_op jit(solution)/shard_map/reduce_scatter | solution.py:22
  608.1 7.4 %convert_element_type.3 = bf16[384,7168]{1,0:T(8,128)(2,1)} convert(f32[384,7168]{1,0:T(8,128)} %reduce-scatter.2.cloned.1.call-done) | non-fusion elementwise | flops 2752512 | bytes 16515072 | tf_op jit(solution)/shard_map/convert_element_type | solution.py:23
  (1 shorter events, 0.0 us)
Async XLA Ops:
  6.5 50.0 %all-gather.3.cloned.1.call-start = ((), (), s32[]{:S(2)}) async-start(), calls=%async_computation.1 | async-start | bytes 4718592 | tf_op jit(solution)/shard_map/all_gather | solution.py:18
  7.3 544.0 %all-gather.5.cloned.1.call-start = ((), (), s32[]{:S(2)}) async-start(), calls=%async_computation.2 | async-start | bytes 36700160 | tf_op jit(solution)/shard_map/all_gather | solution.py:20
  8.0 600.1 %reduce-scatter.2.cloned.1.call-start = ((), (), s32[]{:S(2)}) async-start(), calls=%async_computation.3 | async-start | bytes 33030144 | tf_op jit(solution)/shard_map/reduce_scatter | solution.py:22
Sparse Core Ops, SparseCore 0:
  8.9 47.6 all-gather.2
  58.1 493.0 all-gather.4
  581.3 26.7 reduce-scatter.1
where the time goes:
time: 622 us
  waiting for transfers between devices  571 us (92%)
  matrix products  29.9 us (5%)
  between operations  13.8 us (2%)
  other arithmetic  7.36 us (1%)
    all_gather x1, waiting for transfers between devices, shards(): lax.all_gather(weights, 'gx', axis=1, tiled=True)  495 us
    all_gather x1, waiting for transfers between devices, shards(): shard_rows = lax.all_gather(tokens, 'gz', axis=0, tiled=True)  47.8 us
    dot_general x1, matrix products, block_product(): jnp.dot(left_rows, column_piece, preferred_element_type=jnp.float32)  29.9 us
    reduce_scatter x1, waiting for transfers between devices, shards(): lax.psum_scatter(partial_value, 'gy', scatter_dimension=0, tiled=True)  27 us
  transfers between devices with their start and end apart: 3, of which 3 were waited for; matrix products, arithmetic and copies ran while one was open for 0% of the time, Pallas kernels for 0%

commit v1 on v0

--- a/solution.py
+++ b/solution.py
@@ -1,9 +1,14 @@
+import functools
+
 import jax
 import jax.numpy as jnp
 from jax import lax
+from jax.experimental import pallas as pl
+from jax.experimental.pallas import tpu as pltpu
 from jax.sharding import PartitionSpec as P
 
 BLOCK = 128
+MESH = pl.DeviceIdType.MESH
 
 
 def block_product(left_rows, column_piece, valid_count):
@@ -13,7 +18,7 @@
     return jnp.where((row_index < valid_count * BLOCK)[:, None], product, jnp.float32(0.0))
 
 
-def shards(tokens, weights, counts):
+def shards_general(tokens, weights, counts):
     valid_count = counts[0]
     shard_rows = lax.all_gather(tokens, "gz", axis=0, tiled=True)
     partial_value = block_product(
@@ -23,9 +28,203 @@
     return result.astype(jnp.bfloat16)
 
 
+def kernel(n, nb, tile, tokens, weights, out, t, w, o,
+           load_sem, init_send, init_recv, w_load, w_send, w_recv,
+           up_send, down_send, x_send, t_recv, o_send, o_recv, o_copy):
+    z, g, x = lax.axis_index("gx"), lax.axis_index("gy"), lax.axis_index("gz")
+    depth, cols = weights.shape
+    line = g == x
+
+    barrier = pltpu.get_barrier_semaphore()
+    for d in range(1, n):
+        pl.semaphore_signal(barrier, inc=1, device_id={"gx": lax.rem(z + d, n)}, device_id_type=MESH)
+    pl.semaphore_signal(barrier, inc=1, device_id={"gy": 1 - g}, device_id_type=MESH)
+    pl.semaphore_signal(barrier, inc=1, device_id={"gz": 1 - x}, device_id_type=MESH)
+    pl.semaphore_wait(barrier, n + 1)
+
+    my_depth = pl.ds(pl.multiple_of(g * depth, depth), depth)
+
+    def rows(j):
+        return pl.ds(pl.multiple_of(j * BLOCK, BLOCK), BLOCK)
+
+    def load(j):
+        return pltpu.make_async_copy(tokens.at[rows(j)], t.at[z, j, :, my_depth], load_sem.at[j])
+
+    def hand(j):
+        return pltpu.make_async_remote_copy(
+            tokens.at[rows(j)], t.at[z, j, :, my_depth], init_send.at[j], init_recv.at[j],
+            device_id={"gy": 1 - g}, device_id_type=MESH)
+
+    def relay(s, j, sem, where):
+        return pltpu.make_async_remote_copy(
+            t.at[s, j], t.at[s, j], sem.at[s, j], t_recv.at[s, j],
+            device_id=where, device_id_type=MESH)
+
+    def up(s, j):
+        return relay(s, j, up_send, {"gx": jnp.minimum(z + 1, n - 1)})
+
+    def down(s, j):
+        return relay(s, j, down_send, {"gx": jnp.maximum(z - 1, 0)})
+
+    def across(s, j):
+        return relay(s, j, x_send, {"gz": 1 - x})
+
+    def columns(c):
+        return pl.ds(pl.multiple_of(c * cols, cols), cols)
+
+    def give(s, j):
+        return pltpu.make_async_remote_copy(
+            o.at[s, j], out.at[rows(j), columns(z)], o_send.at[s, j], o_recv.at[z, j],
+            device_id={"gx": s}, device_id_type=MESH)
+
+    def take(c, j):
+        return pltpu.make_async_remote_copy(
+            o.at[c, j], out.at[rows(j), columns(c)], o_send.at[c, j], o_recv.at[c, j],
+            device_id={"gx": c}, device_id_type=MESH)
+
+    def keep(j):
+        return pltpu.make_async_copy(o.at[z, j], out.at[rows(j), columns(z)], o_copy.at[j])
+
+    w_mine = pltpu.make_async_copy(weights, w.at[my_depth], w_load)
+    w_other = pltpu.make_async_remote_copy(
+        weights, w.at[my_depth], w_send, w_recv, device_id={"gy": 1 - g}, device_id_type=MESH)
+
+    @pl.when(line)
+    def _():
+        for j in range(nb):
+            load(j).start()
+    @pl.when(jnp.logical_not(line))
+    def _():
+        for j in range(nb):
+            hand(j).start()
+    w_mine.start()
+    w_other.start()
+
+    @pl.when(line)
+    def _():
+        for j in range(nb):
+            load(j).wait()
+            hand(j).wait_recv()
+            @pl.when(z < n - 1)
+            def _():
+                up(z, j).start()
+            @pl.when(z > 0)
+            def _():
+                down(z, j).start()
+            across(z, j).start()
+
+    def multiply(s, j):
+        @pl.loop(0, cols // tile)
+        def _(i):
+            at = pl.ds(pl.multiple_of(i * tile, tile), tile)
+            o[s, j, :, at] = jnp.dot(
+                t[s, j], w[:, at], preferred_element_type=jnp.float32).astype(o.dtype)
+
+    w_mine.wait()
+    w_other.wait()
+
+    per = 2 * nb
+
+    @pl.loop(0, (n - 1) * per)
+    def _(i):
+        d, r = i // per + 1, i % per
+        j = r // 2
+        s = z + d * (1 - 2 * (r % 2))
+
+        @pl.when((s >= 0) & (s < n))
+        def _():
+            across(s, j).wait_recv()
+
+            @pl.when(line)
+            def _():
+                @pl.when((s < z) & (z < n - 1))
+                def _():
+                    up(s, j).start()
+                @pl.when((s > z) & (z > 0))
+                def _():
+                    down(s, j).start()
+                across(s, j).start()
+            multiply(s, j)
+            give(s, j).start()
+
+    @pl.when(jnp.logical_not(line))
+    def _():
+        for j in range(nb):
+            across(z, j).wait_recv()
+
+    @pl.loop(0, nb)
+    def _(j):
+        multiply(z, j)
+        keep(j).start()
+
+    @pl.when(jnp.logical_not(line))
+    def _():
+        for j in range(nb):
+            hand(j).wait_send()
+
+    @pl.loop(0, n * nb)
+    def _(i):
+        s, j = i // nb, i % nb
+
+        @pl.when(line)
+        def _():
+            @pl.when((s <= z) & (z < n - 1))
+            def _():
+                up(s, j).wait_send()
+            @pl.when((s >= z) & (z > 0))
+            def _():
+                down(s, j).wait_send()
+            across(s, j).wait_send()
+
+        @pl.when(s != z)
+        def _():
+            give(s, j).wait_send()
+            take(s, j).wait_recv()
+
+    for j in range(nb):
+        keep(j).wait()
+
+
+def shards_kernel(n, tokens, weights, counts):
+    rows, depth = tokens.shape
+    cols = weights.shape[1]
+    nb = rows // BLOCK
+    dma = pltpu.SemaphoreType.DMA
+    product = pl.pallas_call(
+        functools.partial(kernel, n, nb, 256),
+        out_shape=jax.ShapeDtypeStruct((rows, n * cols), jnp.bfloat16),
+        in_specs=[pl.BlockSpec(memory_space=pl.ANY)] * 2,
+        out_specs=pl.BlockSpec(memory_space=pl.ANY),
+        scratch_shapes=[
+            pltpu.VMEM((n, nb, BLOCK, 2 * depth), jnp.bfloat16),
+            pltpu.VMEM((2 * depth, cols), jnp.bfloat16),
+            pltpu.VMEM((n, nb, BLOCK, cols), jnp.bfloat16),
+            dma((nb,)), dma((nb,)), dma((nb,)),
+            dma, dma, dma,
+            dma((n, nb)), dma((n, nb)), dma((n, nb)), dma((n, nb)),
+            dma((n, nb)), dma((n, nb)), dma((nb,)),
+        ],
+        compiler_params=pltpu.CompilerParams(
+            collective_id=0, has_side_effects=True, vmem_limit_bytes=50 * 2**20),
+    )(tokens, weights)
+    row_index = lax.axis_index("gy") * rows + jnp.arange(rows, dtype=jnp.int32)
+    return jnp.where((row_index < counts[0] * BLOCK)[:, None], product, jnp.bfloat16(0.0))
+
+
+def shards(sizes, tokens, weights, counts):
+    rows, depth = tokens.shape
+    cols = weights.shape[1]
+    n = sizes["gx"]
+    held = 2 * (2 * n * rows * depth + 2 * depth * cols + n * rows * cols)
+    if (sizes["gz"] == 2 and sizes["gy"] == 2 and rows % BLOCK == 0 and cols % 256 == 0
+            and depth % 128 == 0 and held < 45 * 2**20):
+        return shards_kernel(n, tokens, weights, counts)
+    return shards_general(tokens, weights, counts)
+
+
 def solution(mesh):
     return jax.shard_map(
-        shards,
+        functools.partial(shards, dict(mesh.shape)),
         mesh=mesh,
         in_specs=(P(("groups", "gx", "gz"), "gy"), P("gy", ("gz", "gx")), P(("groups", "gx"))),
         out_specs=P(("groups", "gx", "gy"), "gz"),

time: 622 us -> 233 us (0.37)
  the two profiles are of different devices: /device:TPU:0 before, /device:TPU:30 now
where the time goes in v1:
time: 233 us
  Pallas kernels  225 us (97%)
  other arithmetic  5.44 us (2%)
    pallas_call x1, Pallas kernels, shards_kernel(): pl.pallas_call(functools.partial(kernel, n, nb, 256), out_shape=jax.Shape...  225 us
    select_n x1, other arithmetic, shards_kernel(): jnp.where((row_index < counts[0] * BLOCK)[:, None], product, jnp.bfloat16...  5.44 us

profile of v1, /device:TPU:30, one launch (start us, length us, event | category | flops | bytes accessed | tf_op | source)
XLA Modules:
  0.0 232.8 jit_solution(3383633290044658445)
XLA Ops:
  0.7 0.0 copy-start
  0.7 1.4 copy-done
  2.1 225.2 %shard_map.37 = bf16[384,7168]{1,0:T(8,128)(2,1)} custom-call(bf16[384,2048]{1,0:T(8,128)(2,1)S(1)} %copy-done, bf16[2048,1792]{1,0:T(8,128)(2,1)} %weights.1), custom_call_target="tpu_custom_call" | custom-call | tf_op jit(solution)/shard_map/pallas_call | solution.py:193
  227.3 5.4 %broadcast_select_fusion = bf16[384,7168]{1,0:T(8,128)(2,1)} fusion(bf16[384,7168]{1,0:T(8,128)(2,1)} %shard_map.37, pred[384]{0:T(512)(128)(4,1)S(1)} %add_compare_fusion), kind=kLoop, calls=%fused_computation | loop fusion | flops 2752512 | bytes 11010432 | tf_op jit(solution)/shard_map/jit(_where)/select_n | solution.py:211
  (1 shorter events, 0.0 us)
Async XLA Ops:
  0.7 1.4 copy-start

commit v2 on v0

v2 whole, which is shorter than its diff:
```python
import functools

import jax
import jax.numpy as jnp
from jax import lax
from jax.experimental import pallas as pl
from jax.experimental.pallas import tpu as pltpu
from jax.sharding import PartitionSpec as P

BLOCK = 128
LANES = 128
MESH = pl.DeviceIdType.MESH


def block_product(left_rows, column_piece, valid_count):
    total_rows = left_rows.shape[0]
    row_index = jnp.arange(total_rows, dtype=jnp.int32)
    product = jnp.dot(left_rows, column_piece, preferred_element_type=jnp.float32)
    return jnp.where((row_index < valid_count * BLOCK)[:, None], product, jnp.float32(0.0))


def shards_general(tokens, weights, counts):
    valid_count = counts[0]
    shard_rows = lax.all_gather(tokens, "gz", axis=0, tiled=True)
    partial_value = block_product(
        shard_rows, lax.all_gather(weights, "gx", axis=1, tiled=True), valid_count
    )
    result = lax.psum_scatter(partial_value, "gy", scatter_dimension=0, tiled=True)
    return result.astype(jnp.bfloat16)


def kernel(tokens, weights, out, t, wo, wr, oo, op,
           load_sem, tx_send, tz_send, td_send, chip_send, t_recv,
           wo_load, wo_send, wo_recv, wr_send, wr_recv, y_send, y_recv,
           oo_send, op_send, o_recv):
    y, z = lax.axis_index("groups"), lax.axis_index("gx")
    g, x = lax.axis_index("gy"), lax.axis_index("gz")
    rows, depth = tokens.shape
    half = weights.shape[1] // 2
    chunks = half // LANES
    side = z // 2
    role = (z + side) % 2
    mate = 4 * side + 1 - z
    far = 2 - side
    hub = role == 1
    line = g == y

    barrier = pltpu.get_barrier_semaphore()
    for d in range(4):
        for e in range(2):
            if d or e:
                pl.semaphore_signal(barrier, inc=1, device_id={"gx": (z + d) % 4, "gy": (g + e) % 2},
                                    device_id_type=MESH)
    pl.semaphore_signal(barrier, inc=1, device_id={"gz": 1 - x}, device_id_type=MESH)
    pl.semaphore_signal(barrier, inc=1, device_id={"groups": 1 - y}, device_id_type=MESH)
    pl.semaphore_wait(barrier, 9)

    def remote(src, dst, send, recv, **where):
        return pltpu.make_async_remote_copy(src, dst, send, recv, device_id=where, device_id_type=MESH)

    def cut(k):
        return pl.ds(pl.multiple_of(k * depth, depth), depth)

    def slot(r, h, k):
        return t.at[r, h, :, cut(k)]

    own = slot(role, x, g)
    load = pltpu.make_async_copy(tokens, own, load_sem)
    to_x = remote(tokens, own, tx_send, t_recv.at[role, x, g], gz=1 - x)
    to_z = remote(tokens, own, tz_send, t_recv.at[role, x, g], gx=mate)
    relay_x = remote(slot(1 - role, x, g), slot(1 - role, x, g), td_send,
                     t_recv.at[1 - role, x, g], gz=1 - x)

    def to_chip(r, h, k):
        src = tokens if r is role and h is x else slot(r, h, k)
        return remote(src, slot(r, h, k), chip_send.at[r, h], t_recv.at[r, h, k], gy=1 - g)

    def arrived(r, h, k):
        return remote(slot(r, h, k), slot(r, h, k), td_send, t_recv.at[r, h, k], gy=1 - g)

    def part(p):
        return pl.ds(pl.multiple_of(p * half, LANES), half)

    wo_mine = pltpu.make_async_copy(weights.at[:, part(g)], wo.at[cut(g)], wo_load)
    wo_other = remote(weights.at[:, part(1 - g)], wo.at[cut(g)], wo_send, wo_recv, gy=1 - g)

    def lanes(ab):
        return pl.ds(pl.multiple_of(ab * LANES, LANES), LANES)

    def push(i):
        src = weights.at[:, pl.ds(pl.multiple_of(y * half + i * LANES, LANES), LANES)]
        return remote(src, wr.at[i, cut(g), lanes(1 - role)], wr_send.at[i],
                      wr_recv.at[1 - role, i, g], gx=far, gy=y)

    def pushed(ab, i, k):
        dst = wr.at[i, cut(k), lanes(ab)]
        return remote(dst, dst, wr_send.at[i], wr_recv.at[ab, i, k], gy=1 - g)

    def pass_on(ab, i):
        dst = wr.at[i, :, lanes(ab)]
        return remote(dst, dst, y_send.at[ab, i], y_recv.at[ab, i], groups=1 - y)

    def layer(r):
        return (1 - r) * 3 * side + r * (1 + side)

    def own_dst(c, p):
        return out.at[:, pl.ds(pl.multiple_of(c * 2 * half + p * half, LANES), half)]

    def far_layer(ab):
        return (1 - ab) * far + ab * 3 * (1 - side)

    def far_dst(ab, p, i):
        return out.at[:, pl.ds(
            pl.multiple_of(far_layer(ab) * 2 * half + p * half + i * LANES, LANES), LANES)]

    def send_own(r, h):
        return remote(oo.at[r, h], own_dst(z, g), oo_send.at[r, h], o_recv.at[role, g, 0],
                      gx=layer(r), gy=h)

    def keep_own():
        return pltpu.make_async_copy(oo.at[role, g], own_dst(z, g), oo_send.at[role, g])

    def send_far(ab, i, r, h):
        return remote(op.at[i, r, h, :, lanes(ab)], far_dst(ab, g, i), op_send.at[ab, i, r, h],
                      o_recv.at[2 + ab, g, i], gx=layer(r), gy=h)

    def keep_far(ab, i):
        return pltpu.make_async_copy(op.at[i, role, g, :, lanes(ab)], far_dst(ab, g, i),
                                     op_send.at[ab, i, role, g])

    to_x.start()
    to_z.start()
    load.start()
    to_chip(role, x, g).start()

    @pl.loop(0, chunks)
    def _(i):
        push(i).start()
    wo_other.start()
    wo_mine.start()

    def pass_step(ab, i):
        @pl.when(hub & line)
        def _():
            pushed(ab, i, 0).wait_recv()
            pushed(ab, i, 1).wait_recv()
            pass_on(ab, i).start()

    def own_half(r):
        @pl.loop(0, 2)
        def _(h):
            @pl.loop(0, half // 256)
            def _(q):
                at = pl.ds(pl.multiple_of(q * 256, 256), 256)
                oo[r, h, :, at] = jnp.dot(
                    t[r, h], wo[:, at], preferred_element_type=jnp.float32).astype(oo.dtype)
            if half % 256:
                at = pl.ds(half // 256 * 256, half % 256)
                oo[r, h, :, at] = jnp.dot(
                    t[r, h], wo[:, at], preferred_element_type=jnp.float32).astype(oo.dtype)
            mine = (r == role) & (h == g)

            @pl.when(mine)
            def _():
                keep_own().start()

            @pl.when(jnp.logical_not(mine))
            def _():
                send_own(r, h).start()

    def far_pair(i):
        @pl.when(hub)
        def _():
            @pl.when(jnp.logical_not(line))
            def _():
                pass_on(0, i).wait_recv()
                pass_on(1, i).wait_recv()

            @pl.loop(0, 4)
            def _(b):
                r, h = b // 2, b % 2
                op[i, r, h] = jnp.dot(
                    t[r, h], wr[i], preferred_element_type=jnp.float32).astype(op.dtype)
                mine = (r == role) & (h == g)

                @pl.when(mine)
                def _():
                    keep_far(0, i).start()
                    keep_far(1, i).start()

                @pl.when(jnp.logical_not(mine))
                def _():
                    send_far(0, i, r, h).start()
                    send_far(1, i, r, h).start()

    lead = min(3, chunks)
    order = [(0, i) for i in range(lead)]
    for i in range(chunks):
        order.append((1, i))
        if i + lead < chunks:
            order.append((0, i + lead))
    order = order[::-1]

    def next_pass():
        if order:
            pass_step(*order.pop())

    next_pass()
    next_pass()
    arrived(role, 1 - x, g).wait_recv()
    to_chip(role, 1 - x, g).start()
    arrived(1 - role, x, g).wait_recv()
    relay_x.start()
    to_chip(1 - role, x, g).start()
    next_pass()
    load.wait()
    arrived(role, x, 1 - g).wait_recv()
    arrived(role, 1 - x, 1 - g).wait_recv()
    wo_mine.wait()
    wo_other.wait()
    next_pass()
    own_half(role)
    next_pass()
    arrived(1 - role, 1 - x, g).wait_recv()
    to_chip(1 - role, 1 - x, g).start()
    next_pass()
    arrived(1 - role, x, 1 - g).wait_recv()
    arrived(1 - role, 1 - x, 1 - g).wait_recv()
    own_half(1 - role)
    done = 0
    while done < chunks:
        next_pass()
        if (1, done) not in order and (0, done) not in order:
            far_pair(done)
            done += 1

    to_x.wait_send()
    to_z.wait_send()
    relay_x.wait_send()
    for b in range(4):
        to_chip(b // 2, b % 2, g).wait_send()

    @pl.loop(0, 4)
    def _(b):
        r, h = b // 2, b % 2
        mine = (r == role) & (h == g)

        @pl.when(mine)
        def _():
            keep_own().wait()

        @pl.when(jnp.logical_not(mine))
        def _():
            send_own(r, h).wait_send()

        @pl.when(jnp.logical_not(mine))
        def _():
            remote(oo.at[0, 0], own_dst(layer(r), h), oo_send.at[0, 0], o_recv.at[r, h, 0],
                   gy=1 - g).wait_recv()

    @pl.loop(0, chunks)
    def _(i):
        push(i).wait_send()

        @pl.loop(0, 2)
        def _(ab):
            @pl.when(hub & line)
            def _():
                pass_on(ab, i).wait_send()

            @pl.when(hub)
            def _():
                keep_far(ab, i).wait()

                @pl.loop(0, 4)
                def _(b):
                    r, h = b // 2, b % 2

                    @pl.when(jnp.logical_not((r == role) & (h == g)))
                    def _():
                        send_far(ab, i, r, h).wait_send()

            @pl.loop(0, 2)
            def _(p):
                @pl.when(jnp.logical_not(hub & (p == g)))
                def _():
                    remote(op.at[0, 0, 0, :, lanes(0)], far_dst(ab, p, i), op_send.at[0, 0, 0, 0],
                           o_recv.at[2 + ab, p, i], gy=1 - g).wait_recv()


def shards_kernel(tokens, weights, counts):
    rows, depth = tokens.shape
    cols = weights.shape[1]
    half = cols // 2
    chunks = half // LANES
    dma = pltpu.SemaphoreType.DMA
    product = pl.pallas_call(
        kernel,
        out_shape=jax.ShapeDtypeStruct((rows, 4 * cols), jnp.bfloat16),
        in_specs=[pl.BlockSpec(memory_space=pl.ANY)] * 2,
        out_specs=pl.BlockSpec(memory_space=pl.ANY),
        scratch_shapes=[
            pltpu.VMEM((2, 2, rows, 2 * depth), jnp.bfloat16),
            pltpu.VMEM((2 * depth, half), jnp.bfloat16),
            pltpu.VMEM((chunks, 2 * depth, 2 * LANES), jnp.bfloat16),
            pltpu.VMEM((2, 2, rows, half), jnp.bfloat16),
            pltpu.VMEM((chunks, 2, 2, rows, 2 * LANES), jnp.bfloat16),
            dma, dma, dma, dma, dma((2, 2)), dma((2, 2, 2)),
            dma, dma, dma, dma((chunks,)), dma((2, chunks, 2)), dma((2, chunks)), dma((2, chunks)),
            dma((2, 2)), dma((2, chunks, 2, 2)), dma((4, 2, chunks)),
        ],
        compiler_params=pltpu.CompilerParams(
            collective_id=0, has_side_effects=True, vmem_limit_bytes=60 * 2**20),
    )(tokens, weights)
    row_index = lax.axis_index("gy") * rows + jnp.arange(rows, dtype=jnp.int32)
    return jnp.where((row_index < counts[0] * BLOCK)[:, None], product, jnp.bfloat16(0.0))


def shards(sizes, tokens, weights, counts):
    rows, depth = tokens.shape
    cols = weights.shape[1]
    held = 2 * (12 * rows * cols // 2 + 8 * rows * depth + 6 * depth * cols // 2)
    fits = rows % 16 == 0 and cols % (2 * LANES) == 0 and depth % 128 == 0 and held < 56 * 2**20
    if sizes["groups"] == sizes["gy"] == sizes["gz"] == 2 and sizes["gx"] == 4 and fits:
        return shards_kernel(tokens, weights, counts)
    return shards_general(tokens, weights, counts)


def solution(mesh):
    return jax.shard_map(
        functools.partial(shards, dict(mesh.shape)),
        mesh=mesh,
        in_specs=(P(("groups", "gx", "gz"), "gy"), P("gy", ("gz", "gx")), P(("groups", "gx"))),
        out_specs=P(("groups", "gx", "gy"), "gz"),
        check_vma=False,
    )
```

time: 622 us -> 270 us (0.43)
  waiting for transfers between devices: 571 us -> 0 us
  Pallas kernels: 0 us -> 262 us
  matrix products: 29.9 us -> 0 us
  between operations: 13.8 us -> 0.67 us
    all_gather x2 -> x0, waiting for transfers between devices: 543 us -> none  [the longest x1 495 us: shards(): lax.all_gather(weights, 'gx', axis=1, tiled=True)]
    pallas_call x0 -> x1, Pallas kernels: none -> 262 us  [shards_kernel(): pl.pallas_call(kernel, out_shape=jax.ShapeDtypeStruct((rows, 4 * cols), j...]
    dot_general x1 -> x0, matrix products: 29.9 us -> none  [block_product(): jnp.dot(left_rows, column_piece, preferred_element_type=jnp.float32)]
    reduce_scatter x1 -> x0, waiting for transfers between devices: 27 us -> none  [shards(): lax.psum_scatter(partial_value, 'gy', scatter_dimension=0, tiled=True)]
    convert_element_type x1 -> x0, other arithmetic: 7.35 us -> none  [shards(): return result.astype(jnp.bfloat16)]
  transfers between devices with their start and end apart: 3 -> 0, of which waited for: 3 -> 0; matrix products, arithmetic and copies ran while one was open for 0% -> 0% of each run, Pallas kernels for 0% -> 0%
where the time goes in v2:
time: 270 us; the launch traced here: 268 us
  Pallas kernels  262 us (97%)
  other arithmetic  5.44 us (2%)
    pallas_call x1, Pallas kernels, shards_kernel(): pl.pallas_call(kernel, out_shape=jax.ShapeDtypeStruct((rows, 4 * cols), j...  262 us
    select_n x1, other arithmetic, shards_kernel(): jnp.where((row_index < counts[0] * BLOCK)[:, None], product, jnp.bfloat16...  5.44 us

profile of v2, /device:TPU:0, one launch (start us, length us, event | category | flops | bytes accessed | tf_op | source)
XLA Modules:
  0.0 268.2 jit_solution(5956575663886743963)
XLA Ops:
  0.7 262.0 %shard_map.37 = bf16[384,7168]{1,0:T(8,128)(2,1)} custom-call(bf16[384,2048]{1,0:T(8,128)(2,1)} %tokens.1, bf16[2048,1792]{1,0:T(8,128)(2,1)} %weights.1), custom_call_target="tpu_custom_call" | custom-call | tf_op jit(solution)/shard_map/pallas_call | solution.py:297
  262.7 5.4 %broadcast_select_fusion = bf16[384,7168]{1,0:T(8,128)(2,1)} fusion(bf16[384,7168]{1,0:T(8,128)(2,1)} %shard_map.37, pred[384]{0:T(512)(128)(4,1)S(1)} %add_compare_fusion), kind=kLoop, calls=%fused_computation | loop fusion | flops 2752512 | bytes 11010432 | tf_op jit(solution)/shard_map/jit(_where)/select_n | solution.py:316
  (1 shorter events, 0.0 us)

commit v3 on v2

--- a/solution.py
+++ b/solution.py
@@ -168,37 +168,37 @@
             def _():
                 send_own(r, h).start()
 
-    def far_pair(i):
+    def far_one(ab, i):
         @pl.when(hub)
         def _():
             @pl.when(jnp.logical_not(line))
             def _():
-                pass_on(0, i).wait_recv()
-                pass_on(1, i).wait_recv()
+                pass_on(ab, i).wait_recv()
+
+            at = pl.ds(ab * LANES, LANES)
 
             @pl.loop(0, 4)
             def _(b):
                 r, h = b // 2, b % 2
-                op[i, r, h] = jnp.dot(
-                    t[r, h], wr[i], preferred_element_type=jnp.float32).astype(op.dtype)
+                op[i, r, h, :, at] = jnp.dot(
+                    t[r, h], wr[i, :, at], preferred_element_type=jnp.float32).astype(op.dtype)
                 mine = (r == role) & (h == g)
 
                 @pl.when(mine)
                 def _():
-                    keep_far(0, i).start()
-                    keep_far(1, i).start()
+                    keep_far(ab, i).start()
 
                 @pl.when(jnp.logical_not(mine))
                 def _():
-                    send_far(0, i, r, h).start()
-                    send_far(1, i, r, h).start()
-
-    lead = min(3, chunks)
+                    send_far(ab, i, r, h).start()
+
+    lead = max(1, chunks - 1)
     order = [(0, i) for i in range(lead)]
     for i in range(chunks):
         order.append((1, i))
         if i + lead < chunks:
             order.append((0, i + lead))
+    ready = order[::-1]
     order = order[::-1]
 
     def next_pass():
@@ -227,12 +227,11 @@
     arrived(1 - role, x, 1 - g).wait_recv()
     arrived(1 - role, 1 - x, 1 - g).wait_recv()
     own_half(1 - role)
-    done = 0
-    while done < chunks:
+    while ready:
         next_pass()
-        if (1, done) not in order and (0, done) not in order:
-            far_pair(done)
-            done += 1
+        for _ in range(2):
+            if len(ready) > len(order):
+                far_one(*ready.pop())
 
     to_x.wait_send()
     to_z.wait_send()

time: 270 us -> 269 us (level)
  no operation moved by 1% of the time
where the time goes in v3:
time: 269 us
  Pallas kernels  262 us (97%)
  other arithmetic  5.44 us (2%)
    pallas_call x1, Pallas kernels, shards_kernel(): pl.pallas_call(kernel, out_shape=jax.ShapeDtypeStruct((rows, 4 * cols), j...  262 us
    select_n x1, other arithmetic, shards_kernel(): jnp.where((row_index < counts[0] * BLOCK)[:, None], product, jnp.bfloat16...  5.44 us

profile of v3, /device:TPU:0, one launch (start us, length us, event | category | flops | bytes accessed | tf_op | source)
XLA Modules:
  0.0 268.5 jit_solution(4046084807593400354)
XLA Ops:
  0.7 262.4 %shard_map.37 = bf16[384,7168]{1,0:T(8,128)(2,1)} custom-call(bf16[384,2048]{1,0:T(8,128)(2,1)} %tokens.1, bf16[2048,1792]{1,0:T(8,128)(2,1)} %weights.1), custom_call_target="tpu_custom_call" | custom-call | tf_op jit(solution)/shard_map/pallas_call | solution.py:296
  263.1 5.4 %broadcast_select_fusion = bf16[384,7168]{1,0:T(8,128)(2,1)} fusion(bf16[384,7168]{1,0:T(8,128)(2,1)} %shard_map.37, pred[384]{0:T(512)(128)(4,1)S(1)} %add_compare_fusion), kind=kLoop, calls=%fused_computation | loop fusion | flops 2752512 | bytes 11010432 | tf_op jit(solution)/shard_map/jit(_where)/select_n | solution.py:315
  (1 shorter events, 0.0 us)
